TPU v7x, 32 devices: a whole 2x2x4 slice. The times are simulated.
32 devices in a mesh: atom: 8 (over y, x, core), mode: 4 (over z).
Axes of the slice: x: 2, y: 2, z: 4, core: 2. Of those that a mesh axis runs over, the one named last changes fastest.
Arguments:
- features: float32 [128, 8192], P(None, 'atom'), may hold values from -6 to 6
- positions: float32 [3, 8192], P(None, 'atom'), may hold values from 0 to 1, as said below
- wavevectors: int32 [3, 8192], P(None, 'mode'), may hold values from -384 to 384, as said below
- mode_filter: float32 [128, 8192], P(None, 'mode'), may hold values from -12 to 12
- radial_mix: float32 [4, 128, 128], replicated, may hold values from -0.03125 to 0.03125
- radial_rates: float32 [4], replicated, may hold values from 0.2 to 3
- neighbour_ids: int32 [64, 5], P(('atom', 'mode')), may hold values from 0 to 63, as said below
- live_counts: int32 [64], P(('atom', 'mode')), may hold values from 1 to 5, as said below
- cotangent: float32 [128, 8192], P(None, ('atom', 'mode')), may hold values from -6 to 6
Outputs:
- layer_out: float32 [128, 8192], P(None, ('atom', 'mode'))
- grad_features: float32 [128, 8192], P(None, ('atom', 'mode'))
- grad_filter: float32 [128, 8192], P(None, 'mode')
Inputs may be any that keep to these rules, and one draw needn't show every extreme that they name: `positions`: row 0 of atom i lies between b / 64 and (b + 1) / 64, with b = i // 128; rows 1 and 2 lie anywhere in the range. `wavevectors`: row 0 lies between -384 and 384; rows 1 and 2 lie between -12 and 12. `neighbour_ids`: row b lists the 5 blocks (b + o) mod 64, o from -2 to 2, each once, in some order; only the first live_counts[b] slots are live. `live_counts`: some block has all 5 slots live.
All inputs are finite; a program needn't handle non-finite values.
Results may differ from a plain program's by a relative error of at most 0.00035.
Values sent between devices are 32-bit elements; how exact they have to be, the bound alone decides.
A program may use at most 128 MiB of HBM per device.

v0:
```python
import functools

import jax
import jax.numpy as jnp
from jax import lax
from jax.experimental import pallas as pl
from jax.experimental.pallas import tpu as pltpu
from jax.sharding import PartitionSpec as P

BLOCK = 128
REACH = 2
SLOTS = 5
ROWS = 16
VMEM_LIMIT = 56 * 1024 * 1024

SIN_ROOT = (4.442882919124344, -7.308245686508998, 3.606354218431858, -0.8461116503680876, 0.10982451641509068)
COS_ROOT = (1.4142134962552282, -6.978850948563766, 5.73946037690631, -1.8835579059813616, 0.31068802751622054)
SIN_HALF = (3.141592640130707, -5.167710083507862, 2.550077523214134, -0.5982912856178576, 0.0776576603009221)


def horner(coefs, z):
    value = coefs[-1]
    for coef in coefs[-2::-1]:
        value = value * z + coef
    return value


def split(x):
    high = x.astype(jnp.bfloat16)
    return high, (x - high.astype(jnp.float32)).astype(jnp.bfloat16)


def dot3(left, right, dims):
    def one(a, b):
        return lax.dot_general(a, b, (dims, ((), ())), preferred_element_type=jnp.float32)

    return one(left[0], right[0]) + (one(left[0], right[1]) + one(left[1], right[0]))


NN = ((1,), (0,))
NT = ((1,), (1,))
TN = ((0,), (0,))


def forward_kernel(feat_ref, cot_ref, pos_ref, wave_ref, sums_ref, ch_ref, cl_ref, sh_ref, sl_ref, fh, fl):
    channels = feat_ref.shape[0]

    @pl.when(pl.program_id(0) == 0)
    def _():
        for n, ref in enumerate((feat_ref, cot_ref)):
            high, low = split(ref[...])
            fh[n * channels : (n + 1) * channels, :] = high
            fl[n * channels : (n + 1) * channels, :] = low

    tile = wave_ref.shape[0]

    @pl.loop(0, tile // ROWS)
    def _(step):
        rows = pl.ds(pl.multiple_of(step * ROWS, ROWS), ROWS)
        wave = wave_ref[rows, :]
        turns = (
            wave[:, 0:1] * pos_ref[0:1, :] + wave[:, 1:2] * pos_ref[1:2, :] + wave[:, 2:3] * pos_ref[2:3, :]
        )
        r = turns - jnp.round(turns)
        z = r * r
        s = r * horner(SIN_ROOT, z)
        c = horner(COS_ROOT, z)
        ch_ref[rows, :], cl_ref[rows, :] = split(1.0 - s * s)
        sh_ref[rows, :], sl_ref[rows, :] = split(s * c)

    left = (fh[...], fl[...])
    sums_ref[0, : 2 * channels, :] = dot3(left, (ch_ref[...], cl_ref[...]), NT)
    sums_ref[0, 2 * channels :, :] = dot3(left, (sh_ref[...], sl_ref[...]), NT)


def forward_call(features, cotangent, positions, waves, tiles):
    channels, atoms = features.shape
    modes = waves.shape[0]
    tile = modes // tiles
    table = jax.ShapeDtypeStruct((modes, atoms), jnp.bfloat16)
    whole = lambda i: (0, 0)
    return pl.pallas_call(
        forward_kernel,
        grid=(tiles,),
        out_shape=(jax.ShapeDtypeStruct((tiles, 4 * channels, tile), jnp.float32),) + (table,) * 4,
        in_specs=[
            pl.BlockSpec((channels, atoms), whole),
            pl.BlockSpec((channels, atoms), whole),
            pl.BlockSpec(positions.shape, whole),
            pl.BlockSpec((tile, waves.shape[1]), lambda i: (i, 0)),
        ],
        out_specs=[pl.BlockSpec((1, 4 * channels, tile), lambda i: (i, 0, 0))]
        + [pl.BlockSpec((tile, atoms), lambda i: (i, 0))] * 4,
        scratch_shapes=[pltpu.VMEM((2 * channels, atoms), jnp.bfloat16)] * 2,
        compiler_params=pltpu.CompilerParams(vmem_limit_bytes=VMEM_LIMIT),
        cost_estimate=pl.CostEstimate(flops=24 * channels * atoms * modes, bytes_accessed=8 * atoms * modes, transcendentals=0),
        name="forward_sums",
    )(features, cotangent, positions, waves)


def backward_kernel(filt_ref, ch_ref, cl_ref, sh_ref, sl_ref, out_ref):
    half = out_ref.shape[1]
    width = out_ref.shape[2]

    @pl.when(pl.program_id(0) == 0)
    def _():
        out_ref[...] = jnp.zeros_like(out_ref)

    cos_left = split(filt_ref[0, :half, :])
    sin_left = split(filt_ref[0, half : 2 * half, :])
    for q in range(out_ref.shape[0]):
        cols = slice(q * width, (q + 1) * width)
        out_ref[q] += dot3(cos_left, (ch_ref[:, cols], cl_ref[:, cols]), NN) + dot3(
            sin_left, (sh_ref[:, cols], sl_ref[:, cols]), NN
        )


def backward_call(filtered, tables, parts):
    tiles, rows, tile = filtered.shape
    channels = rows // 5
    modes, atoms = tables[0].shape
    return pl.pallas_call(
        backward_kernel,
        grid=(tiles,),
        out_shape=jax.ShapeDtypeStruct((parts, 2 * channels, atoms // parts), jnp.float32),
        in_specs=[pl.BlockSpec((1, rows, tile), lambda i: (i, 0, 0))]
        + [pl.BlockSpec((tile, atoms), lambda i: (i, 0))] * 4,
        out_specs=pl.BlockSpec((parts, 2 * channels, atoms // parts), lambda i: (0, 0, 0)),
        compiler_params=pltpu.CompilerParams(vmem_limit_bytes=VMEM_LIMIT),
        cost_estimate=pl.CostEstimate(flops=24 * channels * atoms * modes, bytes_accessed=8 * atoms * modes, transcendentals=0),
        name="backward_sums",
    )(filtered, *tables)


def short_kernel(total_blocks, near_ref, far_ref, col_ref, row_ref, mix_ref, rate_ref, short_ref, back_ref):
    window = near_ref.shape[1]
    own = row_ref.shape[1]
    lengths = (total_blocks / jnp.pi, 2.0 / jnp.pi, 2.0 / jnp.pi)
    near = split(near_ref[...])
    far = split(far_ref[...])
    reach = window - own + BLOCK
    slots = reach // BLOCK
    for b in range(own // BLOCK):
        mine = slice(b * BLOCK, (b + 1) * BLOCK)
        around = slice(b * BLOCK, b * BLOCK + reach)
        squares = []
        for t in range(slots):
            rows = slice((b + t) * BLOCK, (b + t + 1) * BLOCK)
            total = None
            for d in range(3):
                turn = row_ref[d : d + 1, mine] - col_ref[rows, d : d + 1]
                r = turn - jnp.round(turn)
                term = (lengths[d] * (r * horner(SIN_HALF, r * r))) ** 2
                total = term if total is None else total + term
            squares.append(total)
        short = None
        for n in range(mix_ref.shape[0]):
            rate = rate_ref[n]
            ahead, behind = [], []
            for t in range(slots):
                rows = slice((b + t) * BLOCK, (b + t + 1) * BLOCK)
                weight = jnp.exp(-rate * squares[t])
                ahead.append(weight * row_ref[8 + t : 9 + t, mine])
                behind.append(weight * col_ref[rows, 8 + slots - 1 - t : 8 + slots - t])
            gathered = dot3([x[:, around] for x in near], split(jnp.concatenate(ahead, axis=0)), NN)
            returned = dot3([x[:, around] for x in far], split(jnp.concatenate(behind, axis=0)), NN)
            mix = split(mix_ref[n])
            forth = dot3(mix, split(gathered), TN)
            back = dot3(mix, split(returned), NN)
            short = (forth, back) if short is None else (short[0] + forth, short[1] + back)
        short_ref[:, mine] = short[0]
        back_ref[:, mine] = short[1]


def short_call(near, far, col, row, radial_mix, radial_rates, total_blocks):
    channels, own = near.shape[0], row.shape[1]
    vmem = pl.BlockSpec(memory_space=pltpu.VMEM)
    return pl.pallas_call(
        functools.partial(short_kernel, total_blocks),
        out_shape=(jax.ShapeDtypeStruct((channels, own), jnp.float32),) * 2,
        in_specs=[vmem] * 5 + [pl.BlockSpec(memory_space=pltpu.SMEM)],
        out_specs=[vmem] * 2,
        compiler_params=pltpu.CompilerParams(vmem_limit_bytes=VMEM_LIMIT),
        cost_estimate=pl.CostEstimate(flops=6_000_000_000, bytes_accessed=4_000_000, transcendentals=0),
        name="short_range",
    )(near, far, col, row, radial_mix, radial_rates)


def per_device(features, positions, wavevectors, mode_filter, radial_mix, radial_rates, neighbour_ids, live_counts, cotangent):
    channels, shard_atoms = features.shape
    atom_devices = lax.axis_size("atom")
    mode_devices = lax.axis_size("mode")
    total_atoms = shard_atoms * atom_devices
    inverse_count = 1.0 / total_atoms
    total_blocks = total_atoms // BLOCK
    owned_blocks = neighbour_ids.shape[0]
    owned_rows = owned_blocks * BLOCK
    reach_rows = REACH * BLOCK
    mode_index = lax.axis_index("mode")
    atom_index = lax.axis_index("atom")

    first_own = (atom_index * mode_devices + mode_index) * owned_blocks
    offsets = jnp.mod(
        neighbour_ids - (first_own + jnp.arange(owned_blocks, dtype=jnp.int32))[:, None] + REACH, total_blocks
    )
    live = jnp.arange(SLOTS, dtype=jnp.int32)[None, :] < live_counts[:, None]
    masks = jnp.sum(
        jnp.where(live[:, :, None] & (offsets[:, :, None] == jnp.arange(8, dtype=jnp.int32)), 1.0, 0.0), axis=1
    )
    mask_rows = jnp.repeat(masks.T, BLOCK, axis=1)
    portion = lax.all_gather(jnp.concatenate([cotangent, mask_rows], axis=0), "mode", axis=1, tiled=True)

    stacked = jnp.concatenate([features, portion, jnp.pad(positions, ((0, 5), (0, 0)))], axis=0)
    ring = [(i, (i + 1) % atom_devices) for i in range(atom_devices)]
    before = lax.ppermute(stacked[:, -reach_rows:], "atom", ring)
    after = lax.ppermute(stacked[:, :reach_rows], "atom", [(b, a) for a, b in ring])

    waves = wavevectors.astype(jnp.float32).T
    sums, *tables = forward_call(features, portion[:channels], positions, waves, atom_devices)
    share = lax.psum_scatter(sums, "atom", scatter_dimension=0, tiled=False)

    extended = jnp.concatenate([before, stacked, after], axis=1)
    near_all = lax.dynamic_slice_in_dim(extended, mode_index * owned_rows, owned_rows + 2 * reach_rows, 1)
    small = jnp.concatenate([near_all[2 * channels + 8 :], near_all[2 * channels : 2 * channels + 8]], axis=0)
    short_own, back_short = short_call(
        near_all[:channels],
        near_all[channels : 2 * channels],
        small.T,
        small[:, reach_rows:-reach_rows],
        radial_mix,
        radial_rates,
        total_blocks,
    )

    width = mode_filter.shape[1] // atom_devices
    filter_share = lax.dynamic_slice_in_dim(mode_filter, atom_index * width, width, 1) * inverse_count
    quads = share.reshape(4, channels, width)
    grad_share = (quads[0] * quads[1] + quads[2] * quads[3]) * inverse_count
    filtered = jnp.concatenate([(filter_share[None] * quads).reshape(4 * channels, width), grad_share], axis=0)
    gathered = lax.all_gather(filtered, "atom", axis=0, tiled=False)
    grad_filter = gathered[:, 4 * channels :, :].transpose(1, 0, 2).reshape(channels, -1)

    parts = backward_call(gathered, tables, mode_devices)
    own = lax.psum_scatter(parts, "mode", scatter_dimension=0, tiled=False)
    own_feat = lax.dynamic_slice_in_dim(features, mode_index * owned_rows, owned_rows, 1)
    return (
        own_feat + own[:channels] + short_own,
        cotangent + own[channels:] + back_short,
        grad_filter,
    )


def solution(mesh):
    in_specs = (
        P(None, "atom"),
        P(None, "atom"),
        P(None, "mode"),
        P(None, "mode"),
        P(),
        P(),
        P(("atom", "mode"), None),
        P(("atom", "mode")),
        P(None, ("atom", "mode")),
    )
    out_specs = (P(None, ("atom", "mode")), P(None, ("atom", "mode")), P(None, "mode"))
    return jax.shard_map(per_device, mesh=mesh, in_specs=in_specs, out_specs=out_specs, check_vma=False)
```

profile of v0, /device:TPU:0, one launch (start us, length us, event | category | flops | bytes accessed | tf_op | source)
XLA Modules:
  0.0 206.3 jit_solution(9076737150991329286)
XLA Ops:
  7.2 0.0 reduce-scatter.3.cloned.1.call-start
  7.2 0.7 iota_compare_fusion
  7.9 0.8 and_select_fusion.1
  8.6 0.1 copy.18
  8.7 0.1 fusion.13
  8.8 0.1 broadcast_bitcast_fusion
  8.9 0.8 convert_element_type.5
  9.7 0.9 pad_maximum_fusion.4
  10.6 17.8 %all_gather.9 = f32[136,1024]{1,0:T(8,128)S(1)} all-gather(f32[136,256]{1,0:T(8,128)S(1)} %pad_maximum_fusion.4), channel_id=1, replica_groups=mesh['atom'=8,'mode'=4] {'mode'}, dimensions={1}, use_global_device_ids=true | all-gather | bytes 696320 | tf_op jit(solution)/shard_map/all_gather | solution.py:211
  28.4 0.8 slice.72.cot_ref
  29.2 1.3 copy.19
  30.5 29.4 %forward_sums.1 = (f32[8,512,256]{2,1,0:T(8,128)}, bf16[2048,1024]{1,0:T(8,128)(2,1)}, bf16[2048,1024]{1,0:T(8,128)(2,1)}, bf16[2048,1024]{1,0:T(8,128)(2,1)}, bf16[2048,1024]{1,0:T(8,128)(2,1)}) custom-call(f32[128,1024]{1,0:T(8,128)} %feat_ref.1, f32[128,1024]{1,0:T(8,128)} %slice.72.cot_ref, f32[3,1024]{1,0:T(4,128)} %pos_ref.1, f32[2048,3]{1,0:T(8,128)} %bitcast.29), custom_call_target="tpu_custom_call" | custom-call | flops 6442450944 | bytes 16777216 | tf_op jit(solution)/shard_map/forward_sums/pallas_call | solution.py:82
  60.0 0.0 reduce-scatter.3.cloned.1.call-update
  60.0 0.0 all-gather.3.cloned.1.call-start
  60.1 0.9 dynamic-slice_multiply_fusion
  61.0 51.9 %reduce-scatter.3.cloned.1.call-done = f32[1,512,256]{2,1,0:T(8,128)} async-done(((f32[8,512,256]{2,1,0:T(8,128)}), f32[1,512,256]{2,1,0:T(8,128)}) %reduce-scatter.3.cloned.1.call-update) | async-done | bytes 524304 | tf_op jit(solution)/shard_map/reduce_scatter | solution.py:220
  112.9 1.1 fusion.10
  114.1 1.1 bitcast_multiply_fusion
  115.2 0.9 pad_maximum_fusion
  116.0 0.0 all-gather.3.cloned.1.call-update
  116.1 0.0 reduce-scatter.5.cloned.1.call-start
  116.1 41.1 %all-gather.3.cloned.1.call-done = f32[5120,256]{1,0:T(8,128)} async-done(((f32[640,256]{1,0:T(8,128)}), f32[5120,256]{1,0:T(8,128)}) %all-gather.3.cloned.1.call-update) | async-done | bytes 5242896 | tf_op jit(solution)/shard_map/all_gather | solution.py:240
  157.2 0.0 copy-start.4
  157.2 0.0 copy-start
  157.2 13.4 %backward_sums.1 = f32[4,256,256]{2,1,0:T(8,128)} custom-call(f32[8,640,256]{2,1,0:T(8,128)} %bitcast.30, bf16[2048,1024]{1,0:T(8,128)(2,1)} %get-tuple-element.11.ch_ref, bf16[2048,1024]{1,0:T(8,128)(2,1)} %get-tuple-element.12.cl_ref, bf16[2048,1024]{1,0:T(8,128)(2,1)} %get-tuple-element.13.sh_ref, bf16[2048,1024]{1,0:T(8,128)(2,1)} %get-tuple-element.14.sl_ref), custom_call_target="tpu_custom_call" | custom-call | flops 6442450944 | bytes 16777216 | tf_op jit(solution)/shard_map/backward_sums/pallas_call | solution.py:122
  170.6 0.0 reduce-scatter.5.cloned.1.call-update
  170.7 0.0 copy-done.4
  170.7 0.0 copy-done
  170.7 1.4 collective-permute-start.1
  172.1 0.0 collective-permute-start
  172.1 7.0 %collective-permute-done.1 = f32[272,256]{1,0:T(8,128)S(1)} collective-permute-done((f32[272,256]{1,0:T(8,128)S(1)}, f32[272,256]{1,0:T(8,128)S(1)}, u32[]{:S(2)}, u32[]{:S(2)}) %collective-permute-start.1) | collective-permute-done | bytes 278560 | tf_op jit(solution)/shard_map/ppermute | solution.py:216
  179.1 1.7 collective-permute-done
  180.9 0.2 fusion.1
  181.1 0.9 copy.20.col_ref
  182.1 0.6 fusion.12.row_ref
  182.7 0.9 fusion.16
  183.6 6.6 %short_range.1 = (f32[128,256]{1,0:T(8,128)}, f32[128,256]{1,0:T(8,128)}) custom-call(f32[128,768]{1,0:T(8,128)} %get-tuple-element.28.near_ref, f32[128,768]{1,0:T(8,128)} %get-tuple-element.27.far_ref, f32[768,16]{1,0:T(8,128)} %copy.20.col_ref, f32[16,256]{1,0:T(8,128)} %fusion.12.row_ref, f32[4,128,128]{2,1,0:T(8,128)} %mix_ref.1, f32[4]{0:T(128)} %rate_ref.1), custom_call_target="tpu_custom_call" | custom-call | flops 6000000000 | bytes 4000000 | tf_op jit(solution)/shard_map/short_range/pallas_call | solution.py:178
  190.2 0.0 copy-start.1
  190.2 0.0 copy-start.2
  190.2 0.0 copy-start.3
  190.2 1.4 slice_bitcast_fusion
  191.6 0.3 copy.21
  191.9 1.3 copy.22
  193.2 4.9 %reduce-scatter.5.cloned.1.call-done = f32[1,256,256]{2,1,0:T(8,128)} async-done(((f32[4,256,256]{2,1,0:T(8,128)}), f32[1,256,256]{2,1,0:T(8,128)}) %reduce-scatter.5.cloned.1.call-update) | async-done | bytes 262160 | tf_op jit(solution)/shard_map/reduce_scatter | solution.py:244
  198.1 0.0 copy-done.1
  198.1 0.0 copy-done.2
  198.1 0.0 copy-done.3
  198.1 1.7 fusion.5
  (5 shorter events, 0.1 us)
Async XLA Ops:
  7.2 105.8 %reduce-scatter.3.cloned.1.call-start = ((), (), s32[]{:S(2)}) async-start(), calls=%async_computation.2 | async-start | bytes 4718592 | tf_op jit(solution)/shard_map/reduce_scatter | solution.py:220
  60.0 97.2 %all-gather.3.cloned.1.call-start = ((), (), s32[]{:S(2)}) async-start(), calls=%async_computation.4 | async-start | bytes 5898240 | tf_op jit(solution)/shard_map/all_gather | solution.py:240
  116.1 82.0 %reduce-scatter.5.cloned.1.call-start = ((), (), s32[]{:S(2)}) async-start(), calls=%async_computation.3 | async-start | bytes 1310720 | tf_op jit(solution)/shard_map/reduce_scatter | solution.py:244
  157.2 13.5 %copy-start.4 = (f32[3,1024]{1,0:T(4,128)S(1)}, f32[3,1024]{1,0:T(4,128)}, u32[]{:S(2)}) copy-start(f32[3,1024]{1,0:T(4,128)} %pos_ref.1) | copy-start | bytes 36868
  157.2 13.5 %copy-start = (f32[128,1024]{1,0:T(8,128)S(1)}, f32[128,1024]{1,0:T(8,128)}, u32[]{:S(2)}) copy-start(f32[128,1024]{1,0:T(8,128)} %feat_ref.1) | copy-start | bytes 1572868
  170.7 8.4 %collective-permute-start.1 = (f32[272,256]{1,0:T(8,128)S(1)}, f32[272,256]{1,0:T(8,128)S(1)}, u32[]{:S(2)}, u32[]{:S(2)}) collective-permute-start(f32[272,256]{1,0:T(8,128)S(1)} %get-tuple-element.23), channel_id=1, source_target_pairs={{4,0},{8,4},{12,8},{16,12},{20,16},{24,20},{28,24},{0,28},{5,1},{9... | collective-permute-start | bytes 835592 | tf_op jit(solution)/shard_map/ppermute | solution.py:216
  172.1 8.8 %collective-permute-start = (f32[272,256]{1,0:T(8,128)S(1)}, f32[272,256]{1,0:T(8,128)S(1)}, u32[]{:S(2)}, u32[]{:S(2)}) collective-permute-start(f32[272,256]{1,0:T(8,128)S(1)} %get-tuple-element.24), channel_id=1, source_target_pairs={{0,4},{4,8},{8,12},{12,16},{16,20},{20,24},{24,28},{28,0},{1,5},{5... | collective-permute-start | bytes 835592 | tf_op jit(solution)/shard_map/ppermute | solution.py:215
  190.2 7.9 %copy-start.1 = (f32[128,256]{1,0:T(8,128)S(1)}, f32[128,256]{1,0:T(8,128)}, u32[]{:S(2)}) copy-start(f32[128,256]{1,0:T(8,128)} %param.17) | copy-start | bytes 393220
  190.2 7.9 %copy-start.2 = (f32[128,256]{1,0:T(8,128)S(1)}, f32[128,256]{1,0:T(8,128)}, u32[]{:S(2)}) copy-start(f32[128,256]{1,0:T(8,128)} %get-tuple-element.15) | copy-start | bytes 393220
  190.2 7.9 %copy-start.3 = (f32[128,256]{1,0:T(8,128)S(1)}, f32[128,256]{1,0:T(8,128)}, u32[]{:S(2)}) copy-start(f32[128,256]{1,0:T(8,128)} %get-tuple-element.16) | copy-start | bytes 393220
Sparse Core Ops, SparseCore 0:
  60.1 52.7 reduce-scatter.2
  116.2 40.9 all-gather.2
  170.8 27.2 reduce-scatter.4
where the time goes:
time: 207 us; the launch traced here: 206 us
  waiting for transfers between devices  107 us (52%)
  Pallas kernels  49.4 us (24%)
  blocking collectives  17.8 us (9%)
  between operations  13.9 us (7%)
  other arithmetic  9.79 us (5%)
  local copies, waits for them, and re-layouts  7.28 us (4%)
    reduce_scatter x1, waiting for transfers between devices, per_device(): share = lax.psum_scatter(sums, 'atom', scatter_dimension=0, tiled=False)  51.9 us
    all_gather x1, waiting for transfers between devices, per_device(): gathered = lax.all_gather(filtered, 'atom', axis=0, tiled=False)  41.1 us
    pallas_call x1, Pallas kernels, forward_call(): pl.pallas_call(forward_kernel, grid=(tiles,), out_shape=(jax.ShapeDtypeSt...  29.4 us
    all_gather x1, blocking collectives, per_device(): lax.all_gather(jnp.concatenate([cotangent, mask_rows], axis=0), 'mode', a...  17.8 us
    pallas_call x1, Pallas kernels, backward_call(): pl.pallas_call(backward_kernel, grid=(tiles,), out_shape=jax.ShapeDtypeSt...  13.4 us
    ppermute x1, waiting for transfers between devices, per_device(): lax.ppermute(stacked[:, :reach_rows], 'atom', [(b, a) for a, b in ring])  7.04 us
    pallas_call x1, Pallas kernels, short_call(): pl.pallas_call(functools.partial(short_kernel, total_blocks), out_shape=(...  6.56 us
    reduce_scatter x1, waiting for transfers between devices, per_device(): own = lax.psum_scatter(parts, 'mode', scatter_dimension=0, tiled=False)  4.88 us
  transfers between devices with their start and end apart: 5, of which 5 were waited for; matrix products, arithmetic and copies ran while one was open for 3% of the time, Pallas kernels for 3%

commit v1 on v0

v1 whole, which is shorter than its diff:
```python
import functools

import jax
import jax.numpy as jnp
from jax import lax
from jax.experimental import pallas as pl
from jax.experimental.pallas import tpu as pltpu
from jax.sharding import PartitionSpec as P

BLOCK = 128
REACH = 2
SLOTS = 5
ROWS = 16
VMEM_LIMIT = 56 * 1024 * 1024

SIN_ROOT = (4.442882919124344, -7.308245686508998, 3.606354218431858, -0.8461116503680876, 0.10982451641509068)
COS_ROOT = (1.4142134962552282, -6.978850948563766, 5.73946037690631, -1.8835579059813616, 0.31068802751622054)
SIN_HALF = (3.141592640130707, -5.167710083507862, 2.550077523214134, -0.5982912856178576, 0.0776576603009221)


def horner(coefs, z):
    value = coefs[-1]
    for coef in coefs[-2::-1]:
        value = value * z + coef
    return value


def split(x):
    high = x.astype(jnp.bfloat16)
    return high, (x - high.astype(jnp.float32)).astype(jnp.bfloat16)


def dot3(left, right, dims):
    def one(a, b):
        return lax.dot_general(a, b, (dims, ((), ())), preferred_element_type=jnp.float32)

    return one(left[0], right[0]) + (one(left[0], right[1]) + one(left[1], right[0]))


NN = ((1,), (0,))
NT = ((1,), (1,))
TN = ((0,), (0,))


def bits_of(count):
    return [1 << k for k in range(count.bit_length() - 1)]


def spectral_kernel(
    n, m, scale,
    feat_ref, cot_ref, pos_ref, wave_ref, filt_ref,
    out_ref, grad_ref,
    fh, fl, cots, ch, cl, sh, sl, held, pair_in, halves_in, full,
    z_send, z_recv, c_send, c_recv, r_send, r_recv, g_send, g_recv, k_send, k_recv,
):
    atom = lax.axis_index("atom")
    mode = lax.axis_index("mode")
    channels, atoms = feat_ref.shape
    part = channels // 2
    own = cot_ref.shape[1]
    tile = ch.shape[1]
    bits = bits_of(n)
    core, rest = bits[0], bits[1:]
    orders = (rest, rest[::-1])
    signs = {bit: 1 - 2 * ((atom // bit) % 2) for bit in bits}

    def at(e):
        place = atom
        for bit in bits:
            if e & bit:
                place = place + signs[bit] * bit
        return place

    def share_of(ref, e, h):
        rows = pl.ds(h * part, part)
        if len(ref.shape) == 3:
            return ref.at[at(e), rows, :]
        return ref.at[rows, pl.ds(pl.multiple_of(at(e) * tile, tile), tile)]

    def remote(src, dst, send, recv, where):
        return pltpu.make_async_remote_copy(
            src_ref=src, dst_ref=dst, send_sem=send, recv_sem=recv, device_id=where, device_id_type=pl.DeviceIdType.MESH
        )

    peers = [{"atom": at(bit)} for bit in bits] + [{"mode": lax.rem(mode + r, m)} for r in range(1, m)]
    barrier = pltpu.get_barrier_semaphore()
    for peer in peers:
        pl.semaphore_signal(barrier, inc=1, device_id=peer, device_id_type=pl.DeviceIdType.MESH)
    pl.semaphore_wait(barrier, len(peers))

    gathers = []
    for r in range(1, m):
        gathers.append(remote(cot_ref, cots.at[r - 1], z_send.at[r - 1], z_recv.at[r - 1], {"mode": lax.rem(mode + r, m)}))
        gathers[-1].start()

    def trig(e):
        first = at(e) * tile

        @pl.loop(0, tile // ROWS)
        def _(step):
            rows = pl.ds(pl.multiple_of(step * ROWS, ROWS), ROWS)
            wave = wave_ref[pl.ds(pl.multiple_of(first + step * ROWS, ROWS), ROWS), :]
            turns = (
                wave[:, 0:1] * pos_ref[0:1, :] + wave[:, 1:2] * pos_ref[1:2, :] + wave[:, 2:3] * pos_ref[2:3, :]
            )
            r = turns - jnp.round(turns)
            z = r * r
            s = r * horner(SIN_ROOT, z)
            c = horner(COS_ROOT, z)
            ch[e, rows, :], cl[e, rows, :] = split(1.0 - s * s)
            sh[e, rows, :], sl[e, rows, :] = split(s * c)

    def place(rows_from, value, cols):
        high, low = split(value)
        for h in range(2):
            rows = slice(h * channels + rows_from, h * channels + rows_from + part)
            fh[rows, cols] = high[h * part : (h + 1) * part]
            fl[rows, cols] = low[h * part : (h + 1) * part]

    place(0, feat_ref[...], slice(None))
    place(part, cot_ref[...], pl.ds(pl.multiple_of(mode * own, own), own))

    evens = [e for e in range(n - 2, -1, -2)]
    sequence = [t for e in evens for t in (e + 1, e)]
    ahead = n // 2
    for e in sequence[:ahead]:
        trig(e)
    for r in range(1, m):
        gathers[r - 1].wait_recv()
        sender = lax.rem(mode - r + m, m)
        place(part, cots[r - 1], pl.ds(pl.multiple_of(sender * own, own), own))

    sent = list(gathers)

    def sums(e):
        left = (fh[...], fl[...])
        for k, (high, low) in enumerate(((ch, cl), (sh, sl))):
            result = dot3(left, (high[e], low[e]), NT)
            held[e, 0, k] = result[:channels]
            held[e, 1, k] = result[channels:]

    landing = {}
    for h in range(2):
        live = evens
        for s, bit in enumerate(orders[h]):
            for e in live:
                if not e & bit:
                    landing[h, s, e] = len(landing)
            live = [e for e in live if not e & bit]

    def stage_copy(h, s, e):
        bit = orders[h][s]
        slot = landing[h, s, e & ~bit]
        return remote(held.at[e | bit, h], halves_in.at[slot], r_send.at[slot], r_recv.at[slot], {"atom": at(bit)})

    def advance(h, e):
        for s, bit in enumerate(orders[h]):
            copy = stage_copy(h, s, e)
            if e & bit:
                copy.start()
                sent.append(copy)
                return
            copy.wait_recv()
            held[e, h] += halves_in[landing[h, s, e]]

    for number, e in enumerate(evens):
        if 2 * number >= ahead:
            trig(e + 1)
        sums(e + 1)
        across = remote(held.at[e + 1], pair_in.at[e // 2], c_send.at[e // 2], c_recv.at[e // 2], {"atom": at(core)})
        across.start()
        sent.append(across)
        if 2 * number + 1 >= ahead:
            trig(e)
        sums(e)
        across.wait_recv()
        held[e] += pair_in[e // 2]
        for h in range(2):
            advance(h, e)

    back = [order[::-1] for order in orders]

    def box(h, e):
        return held.at[0, h] if e == 0 else full.at[e, h]

    def half_copy(h, e, bit):
        slot = h * n + (e | bit)
        return remote(box(h, e), full.at[e | bit, h], g_send.at[slot], g_recv.at[slot], {"atom": at(bit)})

    def last_of(h, e):
        return max(p for p, bit in enumerate(back[h]) if e & bit)

    def forward(h, e, first):
        for bit in back[h][first:]:
            copy = half_copy(h, e, bit)
            copy.start()
            sent.append(copy)

    def core_copy(e):
        source = held.at[0] if e == 0 else full.at[e]
        return remote(source, full.at[e | core], k_send.at[e // 2], k_recv.at[e // 2], {"atom": at(core)})

    def arrive(h, e):
        p = last_of(h, e)
        half_copy(h, e & ~back[h][p], back[h][p]).wait_recv()
        forward(h, e, p + 1)

    def give_back(e, first):
        value = held if e == 0 else full
        left = []
        for k in range(2):
            rows = []
            for h in range(2):
                factor = share_of(filt_ref, e, h)[...] * scale
                rows += [factor * value[e, h, k, :part], factor * value[e, h, k, part:]]
            left.append(split(jnp.concatenate(rows, axis=0)))
        for h in range(2):
            share_of(grad_ref, e, h)[...] = (
                value[e, h, 0, :part] * value[e, h, 0, part:] + value[e, h, 1, :part] * value[e, h, 1, part:]
            ) * scale
        for q in range(m):
            chunk = slice(q * own, (q + 1) * own)
            total = dot3(left[0], (ch[e, :, chunk], cl[e, :, chunk]), NN) + dot3(
                left[1], (sh[e, :, chunk], sl[e, :, chunk]), NN
            )
            if first:
                out_ref[q] = total
            else:
                out_ref[q] += total

    for stage in range(len(rest)):
        for h in range(2):
            copy = half_copy(h, 0, back[h][stage])
            copy.start()
            sent.append(copy)
    copy = core_copy(0)
    copy.start()
    sent.append(copy)
    give_back(0, True)

    arrivals = sorted(
        ((h, e) for e in evens if e for h in range(2)), key=lambda x: (bin(x[1]).count("1"), last_of(*x), x[1])
    )
    waiting = 0
    arrived = set()
    for h, e in arrivals:
        arrive(h, e)
        arrived.add((h, e))
        if (1 - h, e) in arrived:
            copy = core_copy(e)
            copy.start()
            sent.append(copy)
            core_copy(waiting).wait_recv()
            give_back(waiting | core, False)
            give_back(e, False)
            waiting = e
    core_copy(waiting).wait_recv()
    give_back(waiting | core, False)
    for copy in sent:
        copy.wait_send()


def spectral_call(features, cotangent, positions, waves, mode_filter, n, m, scale):
    channels, atoms = features.shape
    modes = waves.shape[0]
    tile = modes // n
    own = cotangent.shape[1]
    vmem = pl.BlockSpec(memory_space=pltpu.VMEM)
    dma = pltpu.SemaphoreType.DMA
    table = pltpu.VMEM((n, tile, atoms), jnp.bfloat16)
    slots = 2 * (n // 2 - 1)
    return pl.pallas_call(
        functools.partial(spectral_kernel, n, m, scale),
        out_shape=(
            jax.ShapeDtypeStruct((m, 2 * channels, own), jnp.float32),
            jax.ShapeDtypeStruct(mode_filter.shape, jnp.float32),
        ),
        in_specs=[vmem] * 5,
        out_specs=[vmem] * 2,
        scratch_shapes=[
            pltpu.VMEM((2 * channels, atoms), jnp.bfloat16),
            pltpu.VMEM((2 * channels, atoms), jnp.bfloat16),
            pltpu.VMEM((m - 1, channels, own), jnp.float32),
            table, table, table, table,
            pltpu.VMEM((n, 2, 2, channels, tile), jnp.float32),
            pltpu.VMEM((n // 2, 2, 2, channels, tile), jnp.float32),
            pltpu.VMEM((slots, 2, channels, tile), jnp.float32),
            pltpu.VMEM((n, 2, 2, channels, tile), jnp.float32),
            dma((m - 1,)), dma((m - 1,)),
            dma((n // 2,)), dma((n // 2,)),
            dma((slots,)), dma((slots,)),
            dma((2 * n,)), dma((2 * n,)),
            dma((n // 2,)), dma((n // 2,)),
        ],
        compiler_params=pltpu.CompilerParams(vmem_limit_bytes=VMEM_LIMIT, collective_id=0, has_side_effects=True),
        cost_estimate=pl.CostEstimate(flops=60 * channels * atoms * modes, bytes_accessed=8 * atoms * modes, transcendentals=0),
        name="spectral",
    )(features, cotangent, positions, waves, mode_filter)


def short_kernel(total_blocks, near_ref, far_ref, col_ref, row_ref, mix_ref, rate_ref, short_ref, back_ref):
    window = near_ref.shape[1]
    own = row_ref.shape[1]
    lengths = (total_blocks / jnp.pi, 2.0 / jnp.pi, 2.0 / jnp.pi)
    near = split(near_ref[...])
    far = split(far_ref[...])
    reach = window - own + BLOCK
    slots = reach // BLOCK
    for b in range(own // BLOCK):
        mine = slice(b * BLOCK, (b + 1) * BLOCK)
        around = slice(b * BLOCK, b * BLOCK + reach)
        squares = []
        for t in range(slots):
            rows = slice((b + t) * BLOCK, (b + t + 1) * BLOCK)
            total = None
            for d in range(3):
                turn = row_ref[d : d + 1, mine] - col_ref[rows, d : d + 1]
                r = turn - jnp.round(turn)
                term = (lengths[d] * (r * horner(SIN_HALF, r * r))) ** 2
                total = term if total is None else total + term
            squares.append(total)
        short = None
        for n in range(mix_ref.shape[0]):
            rate = rate_ref[n]
            ahead, behind = [], []
            for t in range(slots):
                rows = slice((b + t) * BLOCK, (b + t + 1) * BLOCK)
                weight = jnp.exp(-rate * squares[t])
                ahead.append(weight * row_ref[8 + t : 9 + t, mine])
                behind.append(weight * col_ref[rows, 8 + slots - 1 - t : 8 + slots - t])
            gathered = dot3([x[:, around] for x in near], split(jnp.concatenate(ahead, axis=0)), NN)
            returned = dot3([x[:, around] for x in far], split(jnp.concatenate(behind, axis=0)), NN)
            mix = split(mix_ref[n])
            forth = dot3(mix, split(gathered), TN)
            back = dot3(mix, split(returned), NN)
            short = (forth, back) if short is None else (short[0] + forth, short[1] + back)
        short_ref[:, mine] = short[0]
        back_ref[:, mine] = short[1]


def short_call(near, far, col, row, radial_mix, radial_rates, total_blocks):
    channels, own = near.shape[0], row.shape[1]
    vmem = pl.BlockSpec(memory_space=pltpu.VMEM)
    return pl.pallas_call(
        functools.partial(short_kernel, total_blocks),
        out_shape=(jax.ShapeDtypeStruct((channels, own), jnp.float32),) * 2,
        in_specs=[vmem] * 5 + [pl.BlockSpec(memory_space=pltpu.SMEM)],
        out_specs=[vmem] * 2,
        compiler_params=pltpu.CompilerParams(vmem_limit_bytes=VMEM_LIMIT),
        cost_estimate=pl.CostEstimate(flops=6_000_000_000, bytes_accessed=4_000_000, transcendentals=0),
        name="short_range",
    )(near, far, col, row, radial_mix, radial_rates)


def per_device(features, positions, wavevectors, mode_filter, radial_mix, radial_rates, neighbour_ids, live_counts, cotangent):
    channels, shard_atoms = features.shape
    atom_devices = lax.axis_size("atom")
    mode_devices = lax.axis_size("mode")
    total_atoms = shard_atoms * atom_devices
    inverse_count = 1.0 / total_atoms
    total_blocks = total_atoms // BLOCK
    owned_blocks = neighbour_ids.shape[0]
    owned_rows = owned_blocks * BLOCK
    reach_rows = REACH * BLOCK
    mode_index = lax.axis_index("mode")
    atom_index = lax.axis_index("atom")

    first_own = (atom_index * mode_devices + mode_index) * owned_blocks
    offsets = jnp.mod(
        neighbour_ids - (first_own + jnp.arange(owned_blocks, dtype=jnp.int32))[:, None] + REACH, total_blocks
    )
    live = jnp.arange(SLOTS, dtype=jnp.int32)[None, :] < live_counts[:, None]
    masks = jnp.sum(
        jnp.where(live[:, :, None] & (offsets[:, :, None] == jnp.arange(8, dtype=jnp.int32)), 1.0, 0.0), axis=1
    )
    mask_rows = jnp.repeat(masks.T, BLOCK, axis=1)
    mine = mode_index * owned_rows
    own_feat = lax.dynamic_slice_in_dim(features, mine, owned_rows, 1)
    own_pos = lax.dynamic_slice_in_dim(positions, mine, owned_rows, 1)
    stacked = jnp.concatenate([own_feat, cotangent, jnp.pad(own_pos, ((0, 5), (0, 0))), mask_rows], axis=0)
    devices = atom_devices * mode_devices
    steps = -(-reach_rows // owned_rows)
    shift = lambda k: lax.ppermute(stacked, ("atom", "mode"), [(i, (i + k) % devices) for i in range(devices)])
    around = [shift(k) for k in range(steps, 0, -1)] + [stacked] + [shift(-k) for k in range(1, steps + 1)]

    waves = wavevectors.astype(jnp.float32).T
    width = mode_filter.shape[1] // atom_devices
    cut = width % 128 != 0
    filters = mode_filter.reshape(channels, atom_devices, width).transpose(1, 0, 2) if cut else mode_filter
    parts, grad_filter = spectral_call(
        features, cotangent, positions, waves, filters, atom_devices, mode_devices, inverse_count
    )
    if cut:
        grad_filter = grad_filter.transpose(1, 0, 2).reshape(channels, -1)

    spare = steps * owned_rows - reach_rows
    window = jnp.concatenate(around, axis=1)[:, spare : spare + owned_rows + 2 * reach_rows]
    small = window[2 * channels :]
    short_own, back_short = short_call(
        window[:channels],
        window[channels : 2 * channels],
        small.T,
        small[:, reach_rows:-reach_rows],
        radial_mix,
        radial_rates,
        total_blocks,
    )

    own = lax.dynamic_index_in_dim(parts, mode_index, 0, keepdims=False)
    for r in range(1, mode_devices):
        chunk = lax.dynamic_index_in_dim(parts, (mode_index + r) % mode_devices, 0, keepdims=False)
        own = own + lax.ppermute(chunk, "mode", [(i, (i + r) % mode_devices) for i in range(mode_devices)])
    half = channels // 2
    return (
        own_feat + jnp.concatenate([own[:half], own[channels : channels + half]], axis=0) + short_own,
        cotangent + jnp.concatenate([own[half:channels], own[channels + half :]], axis=0) + back_short,
        grad_filter,
    )


def solution(mesh):
    in_specs = (
        P(None, "atom"),
        P(None, "atom"),
        P(None, "mode"),
        P(None, "mode"),
        P(),
        P(),
        P(("atom", "mode"), None),
        P(("atom", "mode")),
        P(None, ("atom", "mode")),
    )
    out_specs = (P(None, ("atom", "mode")), P(None, ("atom", "mode")), P(None, "mode"))
    return jax.shard_map(per_device, mesh=mesh, in_specs=in_specs, out_specs=out_specs, check_vma=False)
```

time: 207 us -> 132 us (0.64)
  the two profiles are of different devices: /device:TPU:0 before, /device:TPU:9 now
where the time goes in v1:
time: 132 us
  Pallas kernels  77.1 us (58%)
  waiting for transfers between devices  33 us (25%)
  local copies, waits for them, and re-layouts  13.4 us (10%)
  starting transfers between devices  5.34 us (4%)
  other arithmetic  1.98 us (2%)
    pallas_call x1, Pallas kernels, spectral_call(): pl.pallas_call(functools.partial(spectral_kernel, n, m, scale), out_shape...  70.5 us
    ppermute x3, waiting for transfers between devices, per_device(): lax.ppermute(chunk, 'mode', [(i, (i + r) % mode_devices) for i in range(m...  21.6 us
    ppermute x2, waiting for transfers between devices, per_device(): lax.ppermute(stacked, ('atom', 'mode'), [(i, (i + k) % devices) for i in...  11.4 us
    pallas_call x1, Pallas kernels, short_call(): pl.pallas_call(functools.partial(short_kernel, total_blocks), out_shape=(...  6.54 us
    ppermute x3, starting transfers between devices, per_device(): lax.ppermute(chunk, 'mode', [(i, (i + r) % mode_devices) for i in range(m...  3.82 us
    unnamed x13, local copies, waits for them, and re-layouts  2.68 us
  transfers between devices with their start and end apart: 5, of which 2 were waited for; matrix products, arithmetic and copies ran while one was open for 3% of the time, Pallas kernels for 0%

profile of v1, /device:TPU:9, one launch (start us, length us, event | category | flops | bytes accessed | tf_op | source)
XLA Modules:
  0.0 131.7 jit_solution(9016378295692789720)
XLA Ops:
  0.7 0.8 convert_element_type.5
  1.4 1.3 %copy.29 = f32[3,2048]{0,1:T(8,128)} copy(f32[3,2048]{1,0:T(4,128)S(1)} %convert_element_type.5) | data formatting | bytes 49152 | tf_op jit(solution)/shard_map/convert_element_type | solution.py:386
  2.8 70.5 %spectral.1 = (f32[4,256,256]{2,1,0:T(8,128)}, f32[128,2048]{1,0:T(8,128)}) custom-call(f32[128,1024]{1,0:T(8,128)} %feat_ref.1, f32[128,256]{1,0:T(8,128)} %cot_ref.1, f32[3,1024]{1,0:T(4,128)} %pos_ref.1, f32[2048,3]{1,0:T(8,128)} %bitcast.15, f32[128,2048]{1,0:T(8,128)} %filt_ref.1), custom_call_target="tpu_custom_call" | custom-call | flops 16106127360 | bytes 16777216 | tf_op jit(solution)/shard_map/spectral/pallas_call | solution.py:272
  73.3 1.3 constant_dynamic-slice_fusion.4
  74.6 0.0 copy-start.3
  74.6 0.0 copy-start.2
  74.6 0.0 copy-start.1
  74.6 0.1 copy.31
  74.8 0.2 collective-permute-start
  75.0 0.1 copy.32
  75.2 2.1 %collective-permute-start.1 = (f32[256,256]{0,1:T(8,128)S(1)}, f32[256,256]{0,1:T(8,128)S(1)}, u32[]{:S(2)}, u32[]{:S(2)}) collective-permute-start(f32[256,256]{0,1:T(8,128)S(1)} %bitcast.17), channel_id=1, source_target_pairs={{0,2},{1,3},{2,0},{3,1},{4,6},{5,7},{6,4},{7,5},{8,10},{9,11},{10,... | collective-permute-start | bytes 786440 | tf_op jit(solution)/shard_map/ppermute | solution.py:412
  77.3 0.8 copy.33
  78.1 1.5 %collective-permute-start.2 = (f32[256,256]{0,1:T(8,128)}, f32[256,256]{0,1:T(8,128)S(1)}, u32[]{:S(2)}, u32[]{:S(2)}) collective-permute-start(f32[256,256]{0,1:T(8,128)} %bitcast.4), channel_id=1, source_target_pairs={{0,3},{1,0},{2,1},{3,2},{4,7},{5,4},{6,5},{7,6},{8,11},{9,8},{10,9... | collective-permute-start | bytes 786440 | tf_op jit(solution)/shard_map/ppermute | solution.py:412
  79.6 0.0 copy-done.3
  79.6 0.0 copy-done.2
  79.6 0.1 and_select_fusion.1
  79.7 0.1 copy.34
  79.8 0.1 fusion.4
  79.9 0.1 broadcast_bitcast_fusion
  79.9 0.9 constant_dynamic-slice_fusion.5
  80.9 0.7 constant_dynamic-slice_fusion
  81.5 0.0 copy-done.1
  81.5 0.1 copy.35
  81.7 0.1 copy.36
  81.8 0.1 copy.37
  81.9 0.1 copy.45
  82.0 0.1 pad_maximum_fusion.1
  82.1 0.1 collective-permute-start.4
  82.2 1.4 %collective-permute-start.3 = (f32[272,256]{0,1:T(8,128)S(1)}, f32[272,256]{0,1:T(8,128)S(1)}, u32[]{:S(2)}, u32[]{:S(2)}) collective-permute-start(f32[272,256]{0,1:T(8,128)S(1)} %pad_maximum_fusion.1), channel_id=1, source_target_pairs={{0,1},{1,2},{2,3},{3,4},{4,5},{5,6},{6,7},{7,8},{8,9},{9,10},{10,1... | collective-permute-start | bytes 835592 | tf_op jit(solution)/shard_map/ppermute | solution.py:383
  83.7 0.1 copy.30
  83.8 0.6 pad_maximum_fusion.2.row_ref
  84.4 0.0 collective-permute-done
  84.4 21.6 %collective-permute-done.1 = f32[256,256]{0,1:T(8,128)S(1)} collective-permute-done((f32[256,256]{0,1:T(8,128)S(1)}, f32[256,256]{0,1:T(8,128)S(1)}, u32[]{:S(2)}, u32[]{:S(2)}) %collective-permute-start.1) | collective-permute-done | bytes 262176 | tf_op jit(solution)/shard_map/ppermute | solution.py:412
  106.0 0.0 collective-permute-done.2
  106.0 0.1 fusion.1
  106.1 0.1 fusion.7
  106.2 11.4 %collective-permute-done.4 = f32[272,256]{0,1:T(8,128)S(1)} collective-permute-done((f32[272,256]{0,1:T(8,128)S(1)}, f32[272,256]{0,1:T(8,128)S(1)}, u32[]{:S(2)}, u32[]{:S(2)}) %collective-permute-start.4) | collective-permute-done | bytes 278560 | tf_op jit(solution)/shard_map/ppermute | solution.py:383
  117.6 0.0 collective-permute-done.3
  117.6 0.1 pad_maximum_fusion
  117.7 0.8 slice_bitcast_fusion.col_ref
  118.5 0.1 fusion.6
  118.6 0.9 copy.39.far_ref
  119.5 0.9 copy.38.near_ref
  120.4 6.5 %short_range.1 = (f32[128,256]{1,0:T(8,128)}, f32[128,256]{1,0:T(8,128)}) custom-call(f32[128,768]{1,0:T(8,128)} %copy.38.near_ref, f32[128,768]{1,0:T(8,128)} %copy.39.far_ref, f32[768,16]{1,0:T(8,128)} %slice_bitcast_fusion.col_ref, f32[16,256]{1,0:T(8,128)} %pad_maximum_fusion.2.row_ref, f32[4,128,128]{2,1,0:T(8,128)} %mix_ref.1, f32[4]{0:T(128)} %rate_ref.1), custom_call_target="tpu_custom_call" | custom-call | flops 6000000000 | bytes 4000000 | tf_op jit(solution)/shard_map/short_range/pallas_call | solution.py:344
  127.0 0.0 copy-start
  127.0 1.1 copy.40
  128.0 1.0 copy.42
  129.1 0.1 fusion.2
  129.2 0.8 copy.43
  130.0 0.8 copy.44
  130.7 0.0 copy-done
  130.7 1.0 copy.47
  (3 shorter events, 0.0 us)
Async XLA Ops:
  74.6 5.0 %copy-start.3 = (s32[2]{0:T(128)S(1)}, s32[2]{0:T(128)}, u32[]{:S(2)}) copy-start(s32[2]{0:T(128)} %param.16) | copy-start | bytes 28
  74.6 5.0 %copy-start.2 = (s32[2,5]{1,0:T(2,128)S(1)}, s32[2,5]{1,0:T(2,128)}, u32[]{:S(2)}) copy-start(s32[2,5]{1,0:T(2,128)} %param.15) | copy-start | bytes 124
  74.6 6.9 %copy-start.1 = (f32[128,256]{1,0:T(8,128)S(1)}, f32[128,256]{1,0:T(8,128)}, u32[]{:S(2)}) copy-start(f32[128,256]{1,0:T(8,128)} %cot_ref.1) | copy-start | bytes 393220
  74.8 9.6 %collective-permute-start = (f32[256,256]{0,1:T(8,128)S(1)}, f32[256,256]{0,1:T(8,128)S(1)}, u32[]{:S(2)}, u32[]{:S(2)}) collective-permute-start(f32[256,256]{0,1:T(8,128)S(1)} %bitcast.16), channel_id=1, source_target_pairs={{0,1},{1,2},{2,3},{3,0},{4,5},{5,6},{6,7},{7,4},{8,9},{9,10},{10,1... | collective-permute-start | bytes 786440 | tf_op jit(solution)/shard_map/ppermute | solution.py:412
  75.2 30.8 %collective-permute-start.1 = (f32[256,256]{0,1:T(8,128)S(1)}, f32[256,256]{0,1:T(8,128)S(1)}, u32[]{:S(2)}, u32[]{:S(2)}) collective-permute-start(f32[256,256]{0,1:T(8,128)S(1)} %bitcast.17), channel_id=1, source_target_pairs={{0,2},{1,3},{2,0},{3,1},{4,6},{5,7},{6,4},{7,5},{8,10},{9,11},{10,... | collective-permute-start | bytes 786440 | tf_op jit(solution)/shard_map/ppermute | solution.py:412
  78.1 27.9 %collective-permute-start.2 = (f32[256,256]{0,1:T(8,128)}, f32[256,256]{0,1:T(8,128)S(1)}, u32[]{:S(2)}, u32[]{:S(2)}) collective-permute-start(f32[256,256]{0,1:T(8,128)} %bitcast.4), channel_id=1, source_target_pairs={{0,3},{1,0},{2,1},{3,2},{4,7},{5,4},{6,5},{7,6},{8,11},{9,8},{10,9... | collective-permute-start | bytes 786440 | tf_op jit(solution)/shard_map/ppermute | solution.py:412
  82.1 35.5 %collective-permute-start.4 = (f32[272,256]{0,1:T(8,128)S(1)}, f32[272,256]{0,1:T(8,128)S(1)}, u32[]{:S(2)}, u32[]{:S(2)}) collective-permute-start(f32[272,256]{0,1:T(8,128)S(1)} %pad_maximum_fusion.1), channel_id=1, source_target_pairs={{0,31},{1,0},{2,1},{3,2},{4,3},{5,4},{6,5},{7,6},{8,7},{9,8},{10,9... | collective-permute-start | bytes 835592 | tf_op jit(solution)/shard_map/ppermute | solution.py:383
  82.2 35.4 %collective-permute-start.3 = (f32[272,256]{0,1:T(8,128)S(1)}, f32[272,256]{0,1:T(8,128)S(1)}, u32[]{:S(2)}, u32[]{:S(2)}) collective-permute-start(f32[272,256]{0,1:T(8,128)S(1)} %pad_maximum_fusion.1), channel_id=1, source_target_pairs={{0,1},{1,2},{2,3},{3,4},{4,5},{5,6},{6,7},{7,8},{8,9},{9,10},{10,1... | collective-permute-start | bytes 835592 | tf_op jit(solution)/shard_map/ppermute | solution.py:383
  127.0 3.8 %copy-start = (f32[128,2048]{1,0:T(8,128)S(1)}, f32[128,2048]{1,0:T(8,128)}, u32[]{:S(2)}) copy-start(f32[128,2048]{1,0:T(8,128)} %get-tuple-element.34) | copy-start | bytes 3145732

commit v2 on v1

v2 whole, which is shorter than its diff:
```python
import functools

import jax
import jax.numpy as jnp
from jax import lax
from jax.experimental import pallas as pl
from jax.experimental.pallas import tpu as pltpu
from jax.sharding import PartitionSpec as P

BLOCK = 128
REACH = 2
SLOTS = 5
ROWS = 16
VMEM_LIMIT = 56 * 1024 * 1024

SIN_ROOT = (4.442882919124344, -7.308245686508998, 3.606354218431858, -0.8461116503680876, 0.10982451641509068)
COS_ROOT = (1.4142134962552282, -6.978850948563766, 5.73946037690631, -1.8835579059813616, 0.31068802751622054)
SIN_HALF = (3.141592640130707, -5.167710083507862, 2.550077523214134, -0.5982912856178576, 0.0776576603009221)


def horner(coefs, z):
    value = coefs[-1]
    for coef in coefs[-2::-1]:
        value = value * z + coef
    return value


def split(x):
    high = x.astype(jnp.bfloat16)
    return high, (x - high.astype(jnp.float32)).astype(jnp.bfloat16)


def dot3(left, right, dims):
    def one(a, b):
        return lax.dot_general(a, b, (dims, ((), ())), preferred_element_type=jnp.float32)

    return one(left[0], right[0]) + (one(left[0], right[1]) + one(left[1], right[0]))


NN = ((1,), (0,))
NT = ((1,), (1,))
TN = ((0,), (0,))


def short_range(total_blocks, near, far, cols_ref, small, mix_ref, rate_ref, store):
    window = near[0].shape[1]
    own = small.shape[1]
    lengths = (total_blocks / jnp.pi, 2.0 / jnp.pi, 2.0 / jnp.pi)
    reach = window - own + BLOCK
    slots = reach // BLOCK
    base = cols_ref.shape[1] - 16
    for b in range(own // BLOCK):
        mine = slice(b * BLOCK, (b + 1) * BLOCK)
        around = slice(b * BLOCK, b * BLOCK + reach)
        squares = []
        for t in range(slots):
            rows = slice((b + t) * BLOCK, (b + t + 1) * BLOCK)
            total = None
            for d in range(3):
                turn = small[d : d + 1, mine] - cols_ref[rows, base + d : base + d + 1]
                r = turn - jnp.round(turn)
                term = (lengths[d] * (r * horner(SIN_HALF, r * r))) ** 2
                total = term if total is None else total + term
            squares.append(total)
        short = None
        for n in range(mix_ref.shape[0]):
            rate = rate_ref[n]
            ahead, behind = [], []
            for t in range(slots):
                rows = slice((b + t) * BLOCK, (b + t + 1) * BLOCK)
                at = base + 8 + slots - 1 - t
                weight = jnp.exp(-rate * squares[t])
                ahead.append(weight * small[8 + t : 9 + t, mine])
                behind.append(weight * cols_ref[rows, at : at + 1])
            gathered = dot3([x[:, around] for x in near], split(jnp.concatenate(ahead, axis=0)), NN)
            returned = dot3([x[:, around] for x in far], split(jnp.concatenate(behind, axis=0)), NN)
            mix = split(mix_ref[n])
            forth = dot3(mix, split(gathered), TN)
            back = dot3(mix, split(returned), NN)
            short = (forth, back) if short is None else (short[0] + forth, short[1] + back)
        store[0, :, mine] = short[0]
        store[1, :, mine] = short[1]


def bits_of(count):
    return [1 << k for k in range(count.bit_length() - 1)]


def layer_kernel(
    n, m, total_blocks, scale,
    feat_ref, cot_ref, pos_ref, wave_ref, filt_ref, mix_ref, rate_ref, ids_ref, live_ref,
    layer_ref, cotgrad_ref, grad_ref,
    mine, halo, nh, nl, xh, xl, cols_ref, shorts, out_ref, out_in,
    fh, fl, cots, ch, cl, sh, sl, held, pair_in, halves_in, full,
    h_send, h_recv, o_send, o_recv, z_send, z_recv, c_send, c_recv, r_send, r_recv, g_send, g_recv, k_send, k_recv,
):
    atom = lax.axis_index("atom")
    mode = lax.axis_index("mode")
    channels, atoms = feat_ref.shape
    part = channels // 2
    own = cot_ref.shape[1]
    tile = ch.shape[1]
    bits = bits_of(n)
    core, rest = bits[0], bits[1:]
    orders = (rest, rest[::-1])
    signs = {bit: 1 - 2 * ((atom // bit) % 2) for bit in bits}

    def at(e):
        place = atom
        for bit in bits:
            if e & bit:
                place = place + signs[bit] * bit
        return place

    def share_of(ref, e, h):
        rows = pl.ds(h * part, part)
        if len(ref.shape) == 3:
            return ref.at[at(e), rows, :]
        return ref.at[rows, pl.ds(pl.multiple_of(at(e) * tile, tile), tile)]

    def remote(src, dst, send, recv, where):
        return pltpu.make_async_remote_copy(
            src_ref=src, dst_ref=dst, send_sem=send, recv_sem=recv, device_id=where, device_id_type=pl.DeviceIdType.MESH
        )

    def along(k):
        target = lax.rem(atom * m + mode + k + n * m, n * m)
        return {"atom": target // m, "mode": lax.rem(target, m)}

    steps = -(-REACH * BLOCK // own)
    shifts = [k for k in range(-steps, steps + 1) if k]
    peers = [{"atom": at(bit)} for bit in bits] + [{"mode": lax.rem(mode + r, m)} for r in range(1, m)]
    peers += [along(k) for k in shifts]
    barrier = pltpu.get_barrier_semaphore()
    for peer in peers:
        pl.semaphore_signal(barrier, inc=1, device_id=peer, device_id_type=pl.DeviceIdType.MESH)
    pl.semaphore_wait(barrier, len(peers))

    gathers = []
    for r in range(1, m):
        gathers.append(remote(cot_ref, cots.at[r - 1], z_send.at[r - 1], z_recv.at[r - 1], {"mode": lax.rem(mode + r, m)}))
        gathers[-1].start()

    own_cols = pl.ds(pl.multiple_of(mode * own, own), own)
    mine[:channels, :] = feat_ref[:, own_cols]
    mine[channels : 2 * channels, :] = cot_ref[...]
    small_rows = 2 * channels
    mine[small_rows:, :] = jnp.zeros((16, own), jnp.float32)
    mine[small_rows : small_rows + 3, :] = pos_ref[:, own_cols]
    first_own = (atom * m + mode) * (own // BLOCK)
    for b in range(own // BLOCK):
        offsets = [lax.rem(ids_ref[b, t] - first_own - b + REACH + 2 * total_blocks, total_blocks) for t in range(SLOTS)]
        for o in range(SLOTS):
            value = jnp.float32(0.0)
            for t in range(SLOTS):
                value += jnp.where((offsets[t] == o) & (t < live_ref[b]), 1.0, 0.0)
            mine[small_rows + 8 + o : small_rows + 9 + o, b * BLOCK : (b + 1) * BLOCK] = jnp.full((1, BLOCK), value)
    halos = []
    for slot, k in enumerate(shifts):
        halos.append(remote(mine, halo.at[slot], h_send.at[slot], h_recv.at[slot], along(-k)))
        halos[-1].start()

    def neighbourhood():
        for copy in halos:
            copy.wait_recv()
        pieces = [halo[slot] for slot in range(steps)] + [mine[...]] + [halo[slot] for slot in range(steps, 2 * steps)]
        spare = steps * own - REACH * BLOCK
        width = own + 2 * REACH * BLOCK
        near = jnp.concatenate([x[:channels] for x in pieces], axis=1)[:, spare : spare + width]
        far = jnp.concatenate([x[channels : 2 * channels] for x in pieces], axis=1)[:, spare : spare + width]
        nh[...], nl[...] = split(near)
        xh[...], xl[...] = split(far)
        last = jnp.concatenate([x[small_rows + 16 - BLOCK :] for x in pieces], axis=1)[:, spare : spare + width]
        for b in range(width // BLOCK):
            part_cols = slice(b * BLOCK, (b + 1) * BLOCK)
            cols_ref[part_cols, :] = last[:, part_cols].T
        short_range(
            total_blocks, (nh, nl), (xh, xl), cols_ref, mine[small_rows:, :], mix_ref, rate_ref, shorts
        )

    def trig(e):
        first = at(e) * tile

        @pl.loop(0, tile // ROWS)
        def _(step):
            rows = pl.ds(pl.multiple_of(step * ROWS, ROWS), ROWS)
            wave = wave_ref[pl.ds(pl.multiple_of(first + step * ROWS, ROWS), ROWS), :]
            turns = (
                wave[:, 0:1] * pos_ref[0:1, :] + wave[:, 1:2] * pos_ref[1:2, :] + wave[:, 2:3] * pos_ref[2:3, :]
            )
            r = turns - jnp.round(turns)
            z = r * r
            s = r * horner(SIN_ROOT, z)
            c = horner(COS_ROOT, z)
            ch[e, rows, :], cl[e, rows, :] = split(1.0 - s * s)
            sh[e, rows, :], sl[e, rows, :] = split(s * c)

    def place(rows_from, value, cols):
        high, low = split(value)
        for h in range(2):
            rows = slice(h * channels + rows_from, h * channels + rows_from + part)
            fh[rows, cols] = high[h * part : (h + 1) * part]
            fl[rows, cols] = low[h * part : (h + 1) * part]

    place(0, feat_ref[...], slice(None))
    place(part, cot_ref[...], pl.ds(pl.multiple_of(mode * own, own), own))

    evens = [e for e in range(n - 2, -1, -2)]
    sequence = [t for e in evens for t in (e + 1, e)]
    ahead = n // 2
    for e in sequence[:ahead]:
        trig(e)
    for r in range(1, m):
        gathers[r - 1].wait_recv()
        sender = lax.rem(mode - r + m, m)
        place(part, cots[r - 1], pl.ds(pl.multiple_of(sender * own, own), own))

    sent = gathers + halos

    def sums(e):
        left = (fh[...], fl[...])
        for k, (high, low) in enumerate(((ch, cl), (sh, sl))):
            result = dot3(left, (high[e], low[e]), NT)
            held[e, 0, k] = result[:channels]
            held[e, 1, k] = result[channels:]

    landing = {}
    for h in range(2):
        live = evens
        for s, bit in enumerate(orders[h]):
            for e in live:
                if not e & bit:
                    landing[h, s, e] = len(landing)
            live = [e for e in live if not e & bit]

    def stage_copy(h, s, e):
        bit = orders[h][s]
        slot = landing[h, s, e & ~bit]
        return remote(held.at[e | bit, h], halves_in.at[slot], r_send.at[slot], r_recv.at[slot], {"atom": at(bit)})

    def advance(h, e):
        for s, bit in enumerate(orders[h]):
            copy = stage_copy(h, s, e)
            if e & bit:
                copy.start()
                sent.append(copy)
                return
            copy.wait_recv()
            held[e, h] += halves_in[landing[h, s, e]]

    for number, e in enumerate(evens):
        if 2 * number >= ahead:
            trig(e + 1)
        sums(e + 1)
        across = remote(held.at[e + 1], pair_in.at[e // 2], c_send.at[e // 2], c_recv.at[e // 2], {"atom": at(core)})
        across.start()
        sent.append(across)
        if 2 * number + 1 >= ahead:
            trig(e)
        sums(e)
        across.wait_recv()
        held[e] += pair_in[e // 2]
        for h in range(2):
            advance(h, e)

    back = [order[::-1] for order in orders]

    def box(h, e):
        return held.at[0, h] if e == 0 else full.at[e, h]

    def half_copy(h, e, bit):
        slot = h * n + (e | bit)
        return remote(box(h, e), full.at[e | bit, h], g_send.at[slot], g_recv.at[slot], {"atom": at(bit)})

    def last_of(h, e):
        return max(p for p, bit in enumerate(back[h]) if e & bit)

    def forward(h, e, first):
        for bit in back[h][first:]:
            copy = half_copy(h, e, bit)
            copy.start()
            sent.append(copy)

    def core_copy(e):
        source = held.at[0] if e == 0 else full.at[e]
        return remote(source, full.at[e | core], k_send.at[e // 2], k_recv.at[e // 2], {"atom": at(core)})

    def arrive(h, e):
        p = last_of(h, e)
        half_copy(h, e & ~back[h][p], back[h][p]).wait_recv()
        forward(h, e, p + 1)

    def give_back(e, first):
        value = held if e == 0 else full
        left = []
        for k in range(2):
            rows = []
            for h in range(2):
                factor = share_of(filt_ref, e, h)[...] * scale
                rows += [factor * value[e, h, k, :part], factor * value[e, h, k, part:]]
            left.append(split(jnp.concatenate(rows, axis=0)))
        for h in range(2):
            share_of(grad_ref, e, h)[...] = (
                value[e, h, 0, :part] * value[e, h, 0, part:] + value[e, h, 1, :part] * value[e, h, 1, part:]
            ) * scale
        for q in range(m):
            chunk = slice(q * own, (q + 1) * own)
            total = dot3(left[0], (ch[e, :, chunk], cl[e, :, chunk]), NN) + dot3(
                left[1], (sh[e, :, chunk], sl[e, :, chunk]), NN
            )
            if first:
                out_ref[q] = total
            else:
                out_ref[q] += total

    for stage in range(len(rest)):
        for h in range(2):
            copy = half_copy(h, 0, back[h][stage])
            copy.start()
            sent.append(copy)
    copy = core_copy(0)
    copy.start()
    sent.append(copy)
    give_back(0, True)
    neighbourhood()

    arrivals = sorted(
        ((h, e) for e in evens if e for h in range(2)), key=lambda x: (bin(x[1]).count("1"), last_of(*x), x[1])
    )
    waiting = 0
    arrived = set()
    for h, e in arrivals:
        arrive(h, e)
        arrived.add((h, e))
        if (1 - h, e) in arrived:
            copy = core_copy(e)
            copy.start()
            sent.append(copy)
            core_copy(waiting).wait_recv()
            give_back(waiting | core, False)
            give_back(e, False)
            waiting = e
    core_copy(waiting).wait_recv()
    give_back(waiting | core, False)
    chunks = []
    for r in range(1, m):
        target = lax.rem(mode + r, m)
        chunks.append(remote(out_ref.at[target], out_in.at[r - 1], o_send.at[r - 1], o_recv.at[r - 1], {"mode": target}))
        chunks[-1].start()
    for copy in chunks:
        copy.wait_recv()
    for h in range(2):
        rows = slice(h * part, (h + 1) * part)
        for ref, k in ((layer_ref, 0), (cotgrad_ref, 1)):
            block = slice(h * channels + k * part, h * channels + (k + 1) * part)
            total = out_ref[mode, block, :]
            for r in range(1, m):
                total = total + out_in[r - 1, block, :]
            start = k * channels + h * part
            ref[rows, :] = mine[start : start + part, :] + total + shorts[k, rows, :]
    for copy in sent + chunks:
        copy.wait_send()


def layer_call(features, cotangent, positions, waves, filters, radial_mix, radial_rates, ids, live, n, m):
    channels, atoms = features.shape
    modes = waves.shape[0]
    tile = modes // n
    own = cotangent.shape[1]
    steps = -(-REACH * BLOCK // own)
    window = own + 2 * REACH * BLOCK
    rows = 2 * channels + 16
    vmem = pl.BlockSpec(memory_space=pltpu.VMEM)
    smem = pl.BlockSpec(memory_space=pltpu.SMEM)
    dma = pltpu.SemaphoreType.DMA
    f32 = lambda *shape: pltpu.VMEM(shape, jnp.float32)
    b16 = lambda *shape: pltpu.VMEM(shape, jnp.bfloat16)
    slots = 2 * (n // 2 - 1)
    pair = lambda count: [dma((count,)), dma((count,))]
    return pl.pallas_call(
        functools.partial(layer_kernel, n, m, n * atoms // BLOCK, 1.0 / (n * atoms)),
        out_shape=(
            jax.ShapeDtypeStruct((channels, own), jnp.float32),
            jax.ShapeDtypeStruct((channels, own), jnp.float32),
            jax.ShapeDtypeStruct(filters.shape, jnp.float32),
        ),
        in_specs=[vmem] * 6 + [smem] * 3,
        out_specs=[vmem] * 3,
        scratch_shapes=[
            f32(rows, own), f32(2 * steps, rows, own),
            b16(channels, window), b16(channels, window), b16(channels, window), b16(channels, window),
            f32(window, BLOCK), f32(2, channels, own),
            f32(m, 2 * channels, own), f32(m - 1, 2 * channels, own),
            b16(2 * channels, atoms), b16(2 * channels, atoms), f32(m - 1, channels, own),
            b16(n, tile, atoms), b16(n, tile, atoms), b16(n, tile, atoms), b16(n, tile, atoms),
            f32(n, 2, 2, channels, tile), f32(n // 2, 2, 2, channels, tile),
            f32(slots, 2, channels, tile), f32(n, 2, 2, channels, tile),
        ]
        + pair(2 * steps) + pair(m - 1) + pair(m - 1) + pair(n // 2) + pair(slots) + pair(2 * n) + pair(n // 2),
        compiler_params=pltpu.CompilerParams(vmem_limit_bytes=VMEM_LIMIT, collective_id=0, has_side_effects=True),
        name="layer",
    )(features, cotangent, positions, waves, filters, radial_mix, radial_rates, ids, live)


def per_device(features, positions, wavevectors, mode_filter, radial_mix, radial_rates, neighbour_ids, live_counts, cotangent):
    channels = features.shape[0]
    n = lax.axis_size("atom")
    m = lax.axis_size("mode")
    waves = wavevectors.astype(jnp.float32).T
    width = mode_filter.shape[1] // n
    cut = width % 128 != 0
    filters = mode_filter.reshape(channels, n, width).transpose(1, 0, 2) if cut else mode_filter
    layer_out, grad_features, grad_filter = layer_call(
        features, cotangent, positions, waves, filters, radial_mix, radial_rates, neighbour_ids, live_counts, n, m
    )
    if cut:
        grad_filter = grad_filter.transpose(1, 0, 2).reshape(channels, -1)
    return layer_out, grad_features, grad_filter


def solution(mesh):
    in_specs = (
        P(None, "atom"),
        P(None, "atom"),
        P(None, "mode"),
        P(None, "mode"),
        P(),
        P(),
        P(("atom", "mode"), None),
        P(("atom", "mode")),
        P(None, ("atom", "mode")),
    )
    out_specs = (P(None, ("atom", "mode")), P(None, ("atom", "mode")), P(None, "mode"))
    return jax.shard_map(per_device, mesh=mesh, in_specs=in_specs, out_specs=out_specs, check_vma=False)
```

time: 132 us -> 108 us (0.82)
  waiting for transfers between devices: 33 us -> 0 us
  Pallas kernels: 77.1 us -> 99.5 us
  local copies, waits for them, and re-layouts: 13.4 us -> 5.9 us
  starting transfers between devices: 5.34 us -> 0 us
    ppermute x5 -> x0, waiting for transfers between devices: 33 us -> none  [the longest x3 21.6 us: per_device(): lax.ppermute(chunk, 'mode', [(i, (i + r) % mode_devices) for i in range(m...]
    pallas_call x2 -> x1, Pallas kernels: 77.1 us -> 99.5 us  [layer_call(): pl.pallas_call(functools.partial(layer_kernel, n, m, n * atoms // BLOCK,...]
    ppermute x5 -> x0, starting transfers between devices: 5.34 us -> none  [the longest x3 3.82 us: per_device(): lax.ppermute(chunk, 'mode', [(i, (i + r) % mode_devices) for i in range(m...]
    dynamic_slice x7 -> x0, local copies, waits for them, and re-layouts: 4.11 us -> none  [the longest x2 1.4 us: per_device(): own = lax.dynamic_index_in_dim(parts, mode_index, 0, keepdims=False)]
    pallas_call x2 -> x0, local copies, waits for them, and re-layouts: 2.08 us -> none  [short_call(): pl.pallas_call(functools.partial(short_kernel, total_blocks), out_shape=(...]
    slice x4 -> x0, local copies, waits for them, and re-layouts: 2.03 us -> none  [the longest x2 0.98 us: per_device(): window[channels:2 * channels]]
    unnamed x13 -> x5, local copies, waits for them, and re-layouts: 2.68 us -> 4.56 us
  transfers between devices with their start and end apart: 5 -> 0, of which waited for: 2 -> 0; matrix products, arithmetic and copies ran while one was open for 3% -> 0% of each run, Pallas kernels for 0% -> 0%
where the time goes in v2:
time: 108 us; the launch traced here: 107 us
  Pallas kernels  99.5 us (92%)
  local copies, waits for them, and re-layouts  5.9 us (5%)
    pallas_call x1, Pallas kernels, layer_call(): pl.pallas_call(functools.partial(layer_kernel, n, m, n * atoms // BLOCK,...  99.5 us
    unnamed x5, local copies, waits for them, and re-layouts  4.56 us

profile of v2, /device:TPU:9, one launch (start us, length us, event | category | flops | bytes accessed | tf_op | source)
XLA Modules:
  0.0 106.8 jit_solution(2099369147807653448)
XLA Ops:
  0.6 0.8 convert_element_type.3
  1.4 1.3 %copy.12 = f32[3,2048]{0,1:T(8,128)} copy(f32[3,2048]{1,0:T(4,128)S(1)} %convert_element_type.3) | data formatting | bytes 49152 | tf_op jit(solution)/shard_map/convert_element_type | solution.py:409
  2.7 99.5 %layer.1 = (f32[128,256]{1,0:T(8,128)}, f32[128,256]{1,0:T(8,128)}, f32[128,2048]{1,0:T(8,128)}) custom-call(f32[128,1024]{1,0:T(8,128)} %feat_ref.1, f32[128,256]{1,0:T(8,128)} %cot_ref.1, f32[3,1024]{1,0:T(4,128)} %pos_ref.1, f32[2048,3]{1,0:T(8,128)} %bitcast.1, f32[128,2048]{1,0:T(8,128)} %filt_ref.1, f32[4,128,128]{2,1,0:T(8,128)} %mix_ref.1, ...), custom_call_target="tpu_custom_call" | custom-call | tf_op jit(solution)/shard_map/layer/pallas_call | solution.py:380
  102.2 0.0 copy-start
  102.2 1.6 %copy.16 = f32[128,256]{1,0:T(8,128)} copy(f32[128,256]{1,0:T(8,128)} %get-tuple-element.6) | data formatting | bytes 262144
  103.8 0.0 copy-done
  103.8 0.7 copy.17
  104.5 2.3 %copy.18 = f32[128,2048]{1,0:T(8,128)} copy(f32[128,2048]{1,0:T(8,128)} %get-tuple-element.8) | data formatting | bytes 2097152
Async XLA Ops:
  102.2 1.6 %copy-start = (f32[128,256]{1,0:T(8,128)S(1)}, f32[128,256]{1,0:T(8,128)}, u32[]{:S(2)}) copy-start(f32[128,256]{1,0:T(8,128)} %get-tuple-element.7) | copy-start | bytes 393220

commit v3 on v2

--- a/solution.py
+++ b/solution.py
@@ -155,10 +155,9 @@
             for t in range(SLOTS):
                 value += jnp.where((offsets[t] == o) & (t < live_ref[b]), 1.0, 0.0)
             mine[small_rows + 8 + o : small_rows + 9 + o, b * BLOCK : (b + 1) * BLOCK] = jnp.full((1, BLOCK), value)
-    halos = []
-    for slot, k in enumerate(shifts):
-        halos.append(remote(mine, halo.at[slot], h_send.at[slot], h_recv.at[slot], along(-k)))
-        halos[-1].start()
+    halos = [
+        remote(mine, halo.at[slot], h_send.at[slot], h_recv.at[slot], along(-k)) for slot, k in enumerate(shifts)
+    ]
 
     def neighbourhood():
         for copy in halos:
@@ -178,22 +177,45 @@
             total_blocks, (nh, nl), (xh, xl), cols_ref, mine[small_rows:, :], mix_ref, rate_ref, shorts
         )
 
+    def trig_rows(e, first, step):
+        rows = pl.ds(pl.multiple_of(step * ROWS, ROWS), ROWS)
+        wave = wave_ref[pl.ds(pl.multiple_of(first + step * ROWS, ROWS), ROWS), :]
+        turns = (
+            wave[:, 0:1] * pos_ref[0:1, :] + wave[:, 1:2] * pos_ref[1:2, :] + wave[:, 2:3] * pos_ref[2:3, :]
+        )
+        r = turns - jnp.round(turns)
+        z = r * r
+        s = r * horner(SIN_ROOT, z)
+        c = horner(COS_ROOT, z)
+        ch[e, rows, :], cl[e, rows, :] = split(1.0 - s * s)
+        sh[e, rows, :], sl[e, rows, :] = split(s * c)
+
     def trig(e):
         first = at(e) * tile
 
         @pl.loop(0, tile // ROWS)
         def _(step):
-            rows = pl.ds(pl.multiple_of(step * ROWS, ROWS), ROWS)
-            wave = wave_ref[pl.ds(pl.multiple_of(first + step * ROWS, ROWS), ROWS), :]
-            turns = (
-                wave[:, 0:1] * pos_ref[0:1, :] + wave[:, 1:2] * pos_ref[1:2, :] + wave[:, 2:3] * pos_ref[2:3, :]
-            )
-            r = turns - jnp.round(turns)
-            z = r * r
-            s = r * horner(SIN_ROOT, z)
-            c = horner(COS_ROOT, z)
-            ch[e, rows, :], cl[e, rows, :] = split(1.0 - s * s)
-            sh[e, rows, :], sl[e, rows, :] = split(s * c)
+            trig_rows(e, first, step)
+
+    def sums_and_trig(e, following):
+        slices = 4
+        depth = atoms // slices
+        count = tile // ROWS // slices
+        first = at(following) * tile
+        for k in range(2):
+            held[e, 0, k] = jnp.zeros((channels, tile), jnp.float32)
+            held[e, 1, k] = jnp.zeros((channels, tile), jnp.float32)
+
+        @pl.loop(0, slices)
+        def _(j):
+            cols = pl.ds(pl.multiple_of(j * depth, depth), depth)
+            left = (fh[:, cols], fl[:, cols])
+            for k, (high, low) in enumerate(((ch, cl), (sh, sl))):
+                result = dot3(left, (high[e, :, cols], low[e, :, cols]), NT)
+                held[e, 0, k] += result[:channels]
+                held[e, 1, k] += result[channels:]
+                for i in range(k * count // 2, (k + 1) * count // 2):
+                    trig_rows(following, first, j * count + i)
 
     def place(rows_from, value, cols):
         high, low = split(value)
@@ -215,6 +237,8 @@
         sender = lax.rem(mode - r + m, m)
         place(part, cots[r - 1], pl.ds(pl.multiple_of(sender * own, own), own))
 
+    for copy in halos:
+        copy.start()
     sent = gathers + halos
 
     def sums(e):
@@ -248,16 +272,19 @@
             copy.wait_recv()
             held[e, h] += halves_in[landing[h, s, e]]
 
+    def step_of(number):
+        e, following = sequence[number], number + ahead
+        if following < n:
+            sums_and_trig(e, sequence[following])
+        else:
+            sums(e)
+
     for number, e in enumerate(evens):
-        if 2 * number >= ahead:
-            trig(e + 1)
-        sums(e + 1)
+        step_of(2 * number)
         across = remote(held.at[e + 1], pair_in.at[e // 2], c_send.at[e // 2], c_recv.at[e // 2], {"atom": at(core)})
         across.start()
         sent.append(across)
-        if 2 * number + 1 >= ahead:
-            trig(e)
-        sums(e)
+        step_of(2 * number + 1)
         across.wait_recv()
         held[e] += pair_in[e // 2]
         for h in range(2):
@@ -322,7 +349,6 @@
     copy.start()
     sent.append(copy)
     give_back(0, True)
-    neighbourhood()
 
     arrivals = sorted(
         ((h, e) for e in evens if e for h in range(2)), key=lambda x: (bin(x[1]).count("1"), last_of(*x), x[1])
@@ -347,6 +373,7 @@
         target = lax.rem(mode + r, m)
         chunks.append(remote(out_ref.at[target], out_in.at[r - 1], o_send.at[r - 1], o_recv.at[r - 1], {"mode": target}))
         chunks[-1].start()
+    neighbourhood()
     for copy in chunks:
         copy.wait_recv()
     for h in range(2):

time: 108 us -> 101 us (0.935)
  Pallas kernels: 99.5 us -> 92.4 us
    pallas_call x1, Pallas kernels: 99.5 us -> 92.4 us  [layer_call(): pl.pallas_call(functools.partial(layer_kernel, n, m, n * atoms // BLOCK,...]
where the time goes in v3:
time: 101 us; the launch traced here: 99.7 us
  Pallas kernels  92.4 us (91%)
  local copies, waits for them, and re-layouts  5.9 us (6%)
    pallas_call x1, Pallas kernels, layer_call(): pl.pallas_call(functools.partial(layer_kernel, n, m, n * atoms // BLOCK,...  92.4 us
    unnamed x5, local copies, waits for them, and re-layouts  4.56 us

profile of v3, /device:TPU:9, one launch (start us, length us, event | category | flops | bytes accessed | tf_op | source)
XLA Modules:
  0.0 99.7 jit_solution(10873146848763744985)
XLA Ops:
  0.6 0.8 convert_element_type.3
  1.4 1.3 %copy.12 = f32[3,2048]{0,1:T(8,128)} copy(f32[3,2048]{1,0:T(4,128)S(1)} %convert_element_type.3) | data formatting | bytes 49152 | tf_op jit(solution)/shard_map/convert_element_type | solution.py:436
  2.7 92.4 %layer.1 = (f32[128,256]{1,0:T(8,128)}, f32[128,256]{1,0:T(8,128)}, f32[128,2048]{1,0:T(8,128)}) custom-call(f32[128,1024]{1,0:T(8,128)} %feat_ref.1, f32[128,256]{1,0:T(8,128)} %cot_ref.1, f32[3,1024]{1,0:T(4,128)} %pos_ref.1, f32[2048,3]{1,0:T(8,128)} %bitcast.1, f32[128,2048]{1,0:T(8,128)} %filt_ref.1, f32[4,128,128]{2,1,0:T(8,128)} %mix_ref.1, ...), custom_call_target="tpu_custom_call" | custom-call | tf_op jit(solution)/shard_map/layer/pallas_call | solution.py:407
  95.2 0.0 copy-start
  95.2 1.6 %copy.16 = f32[128,256]{1,0:T(8,128)} copy(f32[128,256]{1,0:T(8,128)} %get-tuple-element.6) | data formatting | bytes 262144
  96.8 0.0 copy-done
  96.8 0.7 copy.17
  97.4 2.3 %copy.18 = f32[128,2048]{1,0:T(8,128)} copy(f32[128,2048]{1,0:T(8,128)} %get-tuple-element.8) | data formatting | bytes 2097152
Async XLA Ops:
  95.2 1.6 %copy-start = (f32[128,256]{1,0:T(8,128)S(1)}, f32[128,256]{1,0:T(8,128)}, u32[]{:S(2)}) copy-start(f32[128,256]{1,0:T(8,128)} %get-tuple-element.7) | copy-start | bytes 393220
